TPU v7x, 512 devices: a whole 4x4x16 slice. The times are simulated.
512 devices in a mesh: layer: 4 (over y), dp: 4 (over x_lo, core), mp: 32 (over z, x_hi).
Axes of the slice: x: 4 (x_hi: 2, x_lo: 2; x = x_hi * 2 + x_lo), y: 4, z: 16, core: 2. Of those that a mesh axis runs over, the one named last changes fastest.
Arguments:
- mlp_in: bfloat16 [4, 128, 2048], P('layer', 'dp', 'mp'), may hold values from -6 to 6
- gate_weight: bfloat16 [4, 2048, 8192], P('layer', None, ('dp', 'mp')), may hold values from -0.125 to 0.125
- up_weight: bfloat16 [4, 2048, 8192], P('layer', None, ('dp', 'mp')), may hold values from -0.125 to 0.125
- down_weight: bfloat16 [4, 8192, 2048], P('layer', ('dp', 'mp')), may hold values from -0.0625 to 0.0625
- enc_weight: bfloat16 [4, 2048, 16384], P('layer', None, ('dp', 'mp')), may hold values from -0.125 to 0.125
- enc_bias: float32 [4, 16384], P('layer', ('dp', 'mp')), may hold values from -3 to 3
- dec_weight: bfloat16 [4, 4, 16384, 2048], P('layer', None, ('dp', 'mp')), may hold values from -0.046875 to 0.046875
Outputs:
- error_nodes: bfloat16 [4, 128, 2048], P('layer', 'dp', 'mp')
- latents: bfloat16 [4, 128, 16384], P('layer', None, ('dp', 'mp'))
All inputs are finite; a program needn't handle non-finite values.
Results may differ from a plain program's by a relative error of at most 0.0049.
Values may be sent and summed in bfloat16 or wider, within the bound.
No kernel may reach another device: no remote copies, remote signals or barrier semaphores. Data moves between devices by JAX's collectives and lax.ppermute only.
A program may use at most 64 MiB of HBM per device.

v0:
```python
import jax
import jax.numpy as jnp
from jax import lax
from jax.sharding import PartitionSpec as P


def choose_source(weights, source, layers):
    return lax.dynamic_index_in_dim(weights, jnp.clip(source, 0, layers - 1), 0, keepdims=False)


def body(mlp_in, gate_weight, up_weight, down_weight, enc_weight, enc_bias, dec_weight):
    layer_now = lax.axis_index("layer")
    layers = lax.axis_size("layer")
    features_full = lax.all_gather(mlp_in, "mp", axis=2, tiled=True)
    tok_rows = features_full.shape[1]
    width = features_full.shape[2]
    gathered = lax.all_gather(features_full.reshape(tok_rows, 1, width), "dp", axis=1, tiled=True)
    spread = gathered.shape[1]
    all_rows = gathered.reshape(tok_rows * spread, width)
    gate_part = jnp.dot(all_rows, gate_weight[0], preferred_element_type=jnp.float32)
    up_part = jnp.dot(all_rows, up_weight[0], preferred_element_type=jnp.float32)
    hidden = (jax.nn.silu(gate_part) * up_part).astype(jnp.bfloat16)
    pre_act = (
        jnp.dot(all_rows, enc_weight[0], preferred_element_type=jnp.float32) + enc_bias[0][None, :]
    )
    latent = jnp.maximum(pre_act, jnp.float32(0.0)).astype(jnp.bfloat16)
    lat_width = latent.shape[1]
    latent_out = (
        latent.reshape(tok_rows, spread, lat_width)
        .transpose(1, 0, 2)
        .reshape(1, tok_rows * spread, lat_width)
    )
    every_layer = lax.all_gather(latent[None], "layer", axis=0, tiled=True)
    keep_mask = (lax.iota(jnp.int32, layers) <= layer_now).astype(jnp.bfloat16)
    stacked = every_layer * keep_mask[:, None, None]
    sources = [which for which in range(layers)]
    latent_cat = jnp.concatenate([stacked[which] for which in range(layers)], axis=1)
    weight_cat = jnp.concatenate(
        [choose_source(dec_weight[0], sources[which], layers) for which in range(layers)], axis=0
    )
    partial_value = jnp.dot(hidden, down_weight[0], preferred_element_type=jnp.float32)
    partial_value = partial_value - jnp.dot(
        latent_cat, weight_cat, preferred_element_type=jnp.float32
    )
    summed = lax.psum_scatter(
        partial_value.reshape(tok_rows, spread * width),
        ("dp", "mp"),
        scatter_dimension=1,
        tiled=True,
    )
    error_out = summed.astype(jnp.bfloat16).reshape(1, tok_rows, -1)
    return (error_out, latent_out)


def solution(mesh):
    return jax.shard_map(
        body,
        mesh=mesh,
        in_specs=(
            P("layer", "dp", "mp"),
            P("layer", None, ("dp", "mp")),
            P("layer", None, ("dp", "mp")),
            P("layer", ("dp", "mp"), None),
            P("layer", None, ("dp", "mp")),
            P("layer", ("dp", "mp")),
            P("layer", None, ("dp", "mp"), None),
        ),
        out_specs=(P("layer", "dp", "mp"), P("layer", None, ("dp", "mp"))),
        check_vma=False,
    )
```

profile of v0, /device:TPU:1, one launch (start us, length us, event | category | flops | bytes accessed | tf_op | source)
XLA Modules:
  0.0 725.2 jit_solution(13167802963294468820)
XLA Ops:
  7.2 0.0 copy-start
  7.2 0.0 copy-start.3
  7.2 0.0 reduce-scatter.4.cloned.1.call-start
  7.3 0.8 copy.15
  8.1 75.4 %all_gather.9 = bf16[1,32,2048]{1,0,2:T(2,128)(2,1)S(1)} all-gather(bf16[1,32,64]{1,0,2:T(2,128)(2,1)S(1)} %copy.15), channel_id=1, replica_groups=mesh['layer'=4,'dp'=4,'mp'=32] {'mp'}, dimensions={2}, use_global_device_ids=true | all-gather | bytes 135168 | tf_op jit(solution)/shard_map/all_gather | solution.py:14
  83.5 0.5 copy.16
  84.0 0.0 copy-start.1
  84.0 0.0 copy-start.2
  84.1 20.7 %all-gather = bf16[1,32,8192]{2,1,0:T(8,128)(2,1)S(1)} all-gather(bf16[1,32,2048]{2,1,0:T(8,128)(2,1)S(1)} %copy.16), channel_id=2, replica_groups=mesh['layer'=4,'dp'=4,'mp'=32] {'dp'}, dimensions={2}, use_global_device_ids=true | all-gather | bytes 655360 | tf_op jit(solution)/shard_map/all_gather | solution.py:17
  104.7 0.4 reshape.36
  105.1 1.2 fusion.15
  106.4 0.0 copy-done
  106.4 0.0 copy-done.3
  106.4 0.3 fusion.8
  106.7 10.0 %all-gather.1 = bf16[512,128]{1,0:T(8,128)(2,1)S(1)} all-gather(bf16[128,128]{1,0:T(8,128)(2,1)S(1)} %fusion.8), channel_id=3, replica_groups=mesh['layer'=4,'dp'=4,'mp'=32] {'layer'}, dimensions={0}, use_global_device_ids=true | all-gather | bytes 163840 | tf_op jit(solution)/shard_map/all_gather | solution.py:33
  116.7 0.1 broadcast_multiply_fusion
  116.8 2.7 slice_bitcast_fusion.3
  119.6 0.0 copy-done.1
  119.6 0.0 copy-done.2
  119.6 0.8 fusion.10
  120.4 1.8 convolution_subtract_fusion
  122.2 0.5 reshape.37
  122.7 2.6 copy.18
  125.4 0.0 reduce-scatter.4.cloned.1.call-update
  125.4 0.6 copy.17
  126.0 590.9 %reduce-scatter.4.cloned.1.call-done = f32[64,32]{1,0:T(8,128)} async-done(((f32[8192,32]{1,0:T(8,128)}), f32[64,32]{1,0:T(8,128)}) %reduce-scatter.4.cloned.1.call-update) | async-done | bytes 8208
  716.9 1.4 copy.19
  (2 shorter events, 0.0 us)
Async XLA Ops:
  7.2 99.2 %copy-start = (bf16[1,2048,128]{2,1,0:T(8,128)(2,1)S(1)}, bf16[1,2048,128]{2,1,0:T(8,128)(2,1)}, u32[]{:S(2)}) copy-start(bf16[1,2048,128]{2,1,0:T(8,128)(2,1)} %param.11) | copy-start | bytes 1572868
  7.2 99.2 %copy-start.3 = (f32[1,128]{1,0:T(1,128)S(1)}, f32[1,128]{1,0:T(1,128)}, u32[]{:S(2)}) copy-start(f32[1,128]{1,0:T(1,128)} %param.12) | copy-start | bytes 1540
  7.2 709.7 %reduce-scatter.4.cloned.1.call-start = ((), (), s32[]{:S(2)}) async-start(), calls=%async_computation.1 | async-start | bytes 4227072
  84.0 35.5 %copy-start.1 = (bf16[1,64,2048]{2,1,0:T(8,128)(2,1)S(1)}, bf16[1,64,2048]{2,1,0:T(8,128)(2,1)}, u32[]{:S(2)}) copy-start(bf16[1,64,2048]{2,1,0:T(8,128)(2,1)} %param.10) | copy-start | bytes 786436
  84.0 35.5 %copy-start.2 = (bf16[1,2048,64]{1,2,0:T(8,128)(2,1)S(1)}, bf16[1,2048,64]{1,2,0:T(8,128)(2,1)}, u32[]{:S(2)}) copy-start(bf16[1,2048,64]{1,2,0:T(8,128)(2,1)} %param.9) | copy-start | bytes 786436
Sparse Core Ops, SparseCore 0:
  125.5 591.3 reduce-scatter.3
where the time goes:
time: 725 us
  waiting for transfers between devices  591 us (82%)
  blocking collectives  106 us (15%)
  between operations  14.1 us (2%)
  local copies, waits for them, and re-layouts  9.71 us (1%)
    unnamed x2, waiting for transfers between devices  591 us
    all_gather x1, blocking collectives, body(): features_full = lax.all_gather(mlp_in, 'mp', axis=2, tiled=True)  75.4 us
    all_gather x1, blocking collectives, body(): lax.all_gather(features_full.reshape(tok_rows, 1, width), 'dp', axis=1, t...  20.7 us
  transfers between devices with their start and end apart: 1, of which 1 were waited for; matrix products, arithmetic and copies ran while one was open for 0% of the time, Pallas kernels for 0%

commit v1 on v0

--- a/solution.py
+++ b/solution.py
@@ -11,7 +11,20 @@
 def body(mlp_in, gate_weight, up_weight, down_weight, enc_weight, enc_bias, dec_weight):
     layer_now = lax.axis_index("layer")
     layers = lax.axis_size("layer")
-    features_full = lax.all_gather(mlp_in, "mp", axis=2, tiled=True)
+
+    def compute_pools_all(q_in):
+        before = jnp.concatenate(
+            lax.all_to_all(
+                jnp.stack([q_in for _ in range(lax.axis_size("mp"))], axis=0),
+                axis_name="mp",
+                split_axis=0,
+                concat_axis=0,
+            ),
+            axis=2,
+        )
+        return before
+
+    features_full = compute_pools_all(mlp_in)
     tok_rows = features_full.shape[1]
     width = features_full.shape[2]
     gathered = lax.all_gather(features_full.reshape(tok_rows, 1, width), "dp", axis=1, tiled=True)

time: 725 us -> 665 us (0.917)
  blocking collectives: 106 us -> 20.1 us
  starting transfers between devices: 0.04 us -> 18.5 us
    all_gather x1 -> x0, blocking collectives: 75.4 us -> none  [body(): features_full = lax.all_gather(mlp_in, 'mp', axis=2, tiled=True)]
    all_to_all x0 -> x1, starting transfers between devices: none -> 18.5 us  [compute_pools_all(): lax.all_to_all(jnp.stack([q_in for _ in range(lax.axis_size('mp'))], axis...]
    all_to_all x0 -> x1, waiting for transfers between devices: none -> 11.9 us  [compute_pools_all(): lax.all_to_all(jnp.stack([q_in for _ in range(lax.axis_size('mp'))], axis...]
    all_gather x1, blocking collectives: 20.7 us -> 10.1 us  [body(): lax.all_gather(features_full.reshape(tok_rows, 1, width), 'dp', axis=1, t...]
  transfers between devices with their start and end apart: 1 -> 2, of which waited for: 1 -> 2; matrix products, arithmetic and copies ran while one was open for 0% -> 1% of each run, Pallas kernels for 0% -> 0%
where the time goes in v1:
time: 665 us
  waiting for transfers between devices  598 us (90%)
  blocking collectives  20.1 us (3%)
  starting transfers between devices  18.5 us (3%)
  between operations  14.2 us (2%)
  local copies, waits for them, and re-layouts  10.7 us (2%)
    unnamed x2, waiting for transfers between devices  586 us
    all_to_all x1, starting transfers between devices, compute_pools_all(): lax.all_to_all(jnp.stack([q_in for _ in range(lax.axis_size('mp'))], axis...  18.5 us
  transfers between devices with their start and end apart: 2, of which 2 were waited for; matrix products, arithmetic and copies ran while one was open for 1% of the time, Pallas kernels for 0%

profile of v1, /device:TPU:1, one launch (start us, length us, event | category | flops | bytes accessed | tf_op | source)
XLA Modules:
  0.0 665.0 jit_solution(835939855945891386)
XLA Ops:
  7.2 0.0 copy-start
  7.2 0.8 stack.2
  8.0 0.8 reshape.47
  8.8 18.5 %all-to-all-start = ((bf16[32,2,1024]{2,1,0:T(2,128)(2,1)}), bf16[32,2,1024]{2,1,0:T(2,128)(2,1)S(1)}, u32[]{:S(2)}, u32[]{:S(2)}) async-start(bf16[32,2,1024]{2,1,0:T(2,128)(2,1)} %reshape.47), calls=%async_computation | async-start | bytes 262144 | tf_op jit(solution)/shard_map/all_to_all | solution.py:17
  27.3 0.0 copy-start.1
  27.3 0.0 reduce-scatter.4.cloned.1.call-start
  27.4 0.0 copy-start.4
  27.4 2.7 slice_bitcast_fusion.3
  30.1 11.9 %all-to-all-done = bf16[32,2,1024]{2,1,0:T(2,128)(2,1)S(1)} async-done(((bf16[32,2,1024]{2,1,0:T(2,128)(2,1)}), bf16[32,2,1024]{2,1,0:T(2,128)(2,1)S(1)}, u32[]{:S(2)}, u32[]{:S(2)}) %all-to-all-start) | async-done | bytes 131104 | tf_op jit(solution)/shard_map/all_to_all | solution.py:17
  42.1 0.2 reshape.48
  42.3 0.1 copy.13
  42.4 0.3 reshape_reshape.3
  42.7 10.1 %all_gather.6 = bf16[32,4,2048]{2,0,1:T(8,128)(2,1)S(1)} all-gather(bf16[32,1,2048]{2,0,1:T(8,128)(2,1)S(1)} %reshape_reshape.3), channel_id=1, replica_groups=mesh['layer'=4,'dp'=4,'mp'=32] {'dp'}, dimensions={1}, use_global_device_ids=true | all-gather | bytes 655360 | tf_op jit(solution)/shard_map/all_gather | solution.py:30
  52.7 0.4 copy.14
  53.2 0.1 reshape.39
  53.3 0.0 copy-done.1
  53.3 0.3 fusion.15
  53.6 0.0 copy-done
  53.6 0.0 copy-done.4
  53.6 0.3 fusion.8
  53.9 10.1 %all-gather = bf16[512,128]{1,0:T(8,128)(2,1)S(1)} all-gather(bf16[128,128]{1,0:T(8,128)(2,1)S(1)} %fusion.8), channel_id=2, replica_groups=mesh['layer'=4,'dp'=4,'mp'=32] {'layer'}, dimensions={0}, use_global_device_ids=true | all-gather | bytes 163840 | tf_op jit(solution)/shard_map/all_gather | solution.py:46
  64.0 0.1 broadcast_multiply_fusion
  64.1 0.0 copy-done.2
  64.1 0.0 copy-done.3
  64.1 0.8 fusion.10
  64.9 1.8 convolution_subtract_fusion
  66.7 0.5 reshape.40
  67.2 2.7 copy.16
  69.9 0.0 reduce-scatter.4.cloned.1.call-update
  69.9 0.6 copy.15
  70.5 586.2 %reduce-scatter.4.cloned.1.call-done = f32[64,32]{1,0:T(8,128)} async-done(((f32[8192,32]{1,0:T(8,128)}), f32[64,32]{1,0:T(8,128)}) %reduce-scatter.4.cloned.1.call-update) | async-done | bytes 8208
  656.7 1.4 copy.17
  (4 shorter events, 0.0 us)
Async XLA Ops:
  7.2 46.4 %copy-start = (bf16[1,2048,128]{2,1,0:T(8,128)(2,1)S(1)}, bf16[1,2048,128]{2,1,0:T(8,128)(2,1)}, u32[]{:S(2)}) copy-start(bf16[1,2048,128]{2,1,0:T(8,128)(2,1)} %param.11) | copy-start | bytes 1572868
  8.8 33.2 %all-to-all-start = ((bf16[32,2,1024]{2,1,0:T(2,128)(2,1)}), bf16[32,2,1024]{2,1,0:T(2,128)(2,1)S(1)}, u32[]{:S(2)}, u32[]{:S(2)}) async-start(bf16[32,2,1024]{2,1,0:T(2,128)(2,1)} %reshape.47), calls=%async_computation | async-start | bytes 262144 | tf_op jit(solution)/shard_map/all_to_all | solution.py:17
  27.3 26.0 %copy-start.1 = (bf16[1,2048,64]{1,2,0:T(8,128)(2,1)S(1)}, bf16[1,2048,64]{1,2,0:T(8,128)(2,1)}, u32[]{:S(2)}) copy-start(bf16[1,2048,64]{1,2,0:T(8,128)(2,1)} %param.8) | copy-start | bytes 786436
  27.3 629.4 %reduce-scatter.4.cloned.1.call-start = ((), (), s32[]{:S(2)}) async-start(), calls=%async_computation.2 | async-start | bytes 4227072
  27.4 26.2 %copy-start.4 = (f32[1,128]{1,0:T(1,128)S(1)}, f32[1,128]{1,0:T(1,128)}, u32[]{:S(2)}) copy-start(f32[1,128]{1,0:T(1,128)} %param.12) | copy-start | bytes 1540
  30.1 34.0 %copy-start.2 = (bf16[1,64,2048]{2,1,0:T(8,128)(2,1)S(1)}, bf16[1,64,2048]{2,1,0:T(8,128)(2,1)}, u32[]{:S(2)}) copy-start(bf16[1,64,2048]{2,1,0:T(8,128)(2,1)} %param.10) | copy-start | bytes 786436
  30.1 34.0 %copy-start.3 = (bf16[1,2048,64]{1,2,0:T(8,128)(2,1)S(1)}, bf16[1,2048,64]{1,2,0:T(8,128)(2,1)}, u32[]{:S(2)}) copy-start(bf16[1,2048,64]{1,2,0:T(8,128)(2,1)} %param.9) | copy-start | bytes 786436
Sparse Core Ops, SparseCore 0:
  70.0 586.6 reduce-scatter.3
